TPU v7x, 32 devices: a whole 2x2x4 slice. The times are simulated.
32 devices in a mesh: slab: 4 (over x, core), grp: 8 (over z, y).
Axes of the slice: x: 2, y: 2, z: 4, core: 2. Of those that a mesh axis runs over, the one named last changes fastest.
Arguments:
- raw_frames: bfloat16 [256, 48, 10752], P('grp', 'slab'), may hold values from -700 to 700
- mask_index: int32 [57344], P(('slab', 'grp')), may hold values from 0 to 516095, as said below
- subspace: bfloat16 [1200, 57344], P(None, ('slab', 'grp')), may hold values from -6 to 6
- rotation: bfloat16 [1456, 1200], replicated, may hold values from -0.15625 to 0.15625
Outputs:
- gram: float32 [1456, 1456], P('grp')
- new_subspace: bfloat16 [1200, 57344], P(None, ('slab', 'grp'))
Inputs may be any that keep to these rules, and one draw needn't show every extreme that they name: `mask_index`: entries are distinct flat grid positions that come in runs of 128 consecutive positions, each run starting at a multiple of 128; the 14336 entries of aligned block s lie in z planes s * 12 to (s + 1) * 12 - 1 and rise within the block; the first 3584 of a block lie in its lowest 3 planes, the last 3584 in its highest 3 planes, the others in the planes between.
All inputs are finite; a program needn't handle non-finite values.
Results may differ from a plain program's by a relative error of at most 0.006.
Values may be sent and summed in bfloat16 or wider, within the bound.
A program may use at most 192 MiB of HBM per device.

v0:
```python
import math
import jax
import jax.numpy as jnp
from jax import lax
from jax.sharding import PartitionSpec as P

NX = 96
RUN = 128
RAD = 3
K = 1200
smooth_sigma = 1.0617
epsilon = 1e-06


def padded_2(cells, sides, width):
    for axis, dim in sides:
        count = lax.axis_size(axis)
        ends = count - 1
        head = lax.slice_in_dim(cells, 0, width, axis=dim)
        tail = lax.slice_in_dim(cells, cells.shape[dim] - width, cells.shape[dim], axis=dim)
        cells = jnp.concatenate(
            [
                lax.ppermute(tail, axis, [(i, (i + 1) % count) for i in range(ends)]),
                cells,
                lax.ppermute(head, axis, [((i + 1) % count, i) for i in range(ends)]),
            ],
            axis=dim,
        )
    return cells


def tap_weights():
    unscaled = [
        math.exp(-offset * offset / (2.0 * smooth_sigma * smooth_sigma))
        for offset in range(-RAD, RAD + 1)
    ]
    summed = sum(unscaled)
    return [weight / summed for weight in unscaled]


def along_rows(volume):
    weights = tap_weights()
    extent = volume.shape[-1]
    column = lax.broadcasted_iota(jnp.int32, (extent,), 0) % NX
    padded = jnp.pad(volume, [(0, 0)] * (volume.ndim - 1) + [(RAD, RAD)])
    summed = jnp.zeros(volume.shape, jnp.float32)
    for offset in range(-RAD, RAD + 1):
        shifted = lax.slice_in_dim(
            padded, RAD + offset, RAD + offset + extent, axis=volume.ndim - 1
        )
        inside = (column + offset >= 0) & (column + offset < NX)
        summed = summed + weights[offset + RAD] * jnp.where(inside, shifted, 0.0)
    return summed


def along_columns(volume):
    weights = tap_weights()
    extent = volume.shape[-1]
    reach_cells = RAD * NX
    padded = jnp.pad(volume, [(0, 0)] * (volume.ndim - 1) + [(reach_cells, reach_cells)])
    summed = jnp.zeros(volume.shape, jnp.float32)
    for offset in range(-RAD, RAD + 1):
        begin = reach_cells + offset * NX
        shifted = lax.slice_in_dim(padded, begin, begin + extent, axis=volume.ndim - 1)
        summed = summed + weights[offset + RAD] * shifted
    return summed


def along_depth(padded, slab_depth):
    weights = tap_weights()
    summed = None
    for offset in range(-RAD, RAD + 1):
        shifted = lax.slice_in_dim(
            padded, RAD + offset, RAD + offset + slab_depth, axis=padded.ndim - 2
        )
        term = weights[offset + RAD] * shifted
        summed = term if summed is None else summed + term
    return summed


def pick_columns(matrix, wanted):
    row_total = matrix.shape[0]
    blocked = matrix.reshape(row_total, matrix.shape[1] // RUN, RUN)
    run_starts = wanted.reshape(-1, RUN)[:, 0] // RUN
    picked_runs = jnp.take(blocked, run_starts, axis=1)
    return picked_runs.reshape(row_total, wanted.shape[0])


def body(raw_frames, mask_index, subspace, rotation):
    frames_here = raw_frames.shape[0]
    slab_depth = raw_frames.shape[1]
    extent = raw_frames.shape[2]
    per_device = subspace.shape[1]
    group_count = lax.axis_size("grp")
    masked = per_device * lax.axis_size("slab") * group_count
    positions = lax.all_gather(mask_index, "grp", axis=0, tiled=True) - lax.axis_index("slab") * (
        slab_depth * extent
    )
    padded = padded_2(raw_frames, (("slab", 1),), RAD)
    planar = along_columns(along_rows(padded.astype(jnp.float32)))
    smoothed = (
        along_depth(planar, slab_depth)
        .reshape(frames_here, slab_depth * extent)
        .astype(jnp.bfloat16)
    )
    picked = pick_columns(smoothed, positions)
    regrouped = lax.all_to_all(picked, "grp", split_axis=1, concat_axis=0, tiled=True)
    frame_count = regrouped.shape[0]
    subject_frames = frame_count // 2
    halves = regrouped.astype(jnp.float32).reshape(2, subject_frames, per_device)
    centered = (halves - jnp.mean(halves, axis=1, keepdims=True)).astype(jnp.bfloat16)
    order_rows = K + frame_count
    stacked = jnp.concatenate([subspace, centered.reshape(frame_count, per_device)], 0)
    widened = centered.astype(jnp.float32)
    power = lax.psum(jnp.sum(widened * widened, axis=(1, 2)), ("slab", "grp"))
    rows_here = order_rows // group_count
    first_row = lax.axis_index("grp") * rows_here
    gram_raw = lax.psum(
        jnp.dot(stacked, stacked.T, preferred_element_type=jnp.float32), ("slab", "grp")
    )
    owned = lax.dynamic_slice_in_dim(gram_raw, first_row, rows_here, 0)
    scales = lax.rsqrt(power / (masked * subject_frames) + epsilon)
    row_scale = jnp.concatenate([jnp.ones((K,), jnp.float32), jnp.repeat(scales, subject_frames)])
    owned_scale = lax.dynamic_slice_in_dim(row_scale, first_row, rows_here, 0)
    gram_rows = owned * (owned_scale[:, None] * row_scale[None, :]) / masked
    contract = (((0,), (0,)), ((), ()))
    from_basis = lax.dot_general(
        rotation[:K], subspace, contract, preferred_element_type=jnp.float32
    )
    from_first = lax.dot_general(
        rotation[K : K + subject_frames], centered[0], contract, preferred_element_type=jnp.float32
    )
    from_second = lax.dot_general(
        rotation[K + subject_frames :], centered[1], contract, preferred_element_type=jnp.float32
    )
    new_subspace = (from_basis + scales[0] * from_first + scales[1] * from_second).astype(
        jnp.bfloat16
    )
    return (gram_rows, new_subspace)


def solution(mesh):
    placed = (P("grp", "slab", None), P(("slab", "grp")), P(None, ("slab", "grp")), P())
    return jax.shard_map(
        body,
        mesh=mesh,
        in_specs=placed,
        out_specs=(P("grp", None), P(None, ("slab", "grp"))),
        check_vma=False,
    )
```

profile of v0, /device:TPU:0, one launch (start us, length us, event | category | flops | bytes accessed | tf_op | source)
XLA Modules:
  0.0 511.2 jit_solution(89150723595462847)
XLA Ops:
  7.2 4.5 fusion.61
  11.7 2.5 collective-permute-start
  14.2 1.3 collective-permute-start.1
  15.5 0.7 reshape.63
  16.2 31.9 %all-gather = s32[8,1,1792]{2,1,0:T(1,128)S(1)} all-gather(s32[1,1,1792]{2,1,0:T(1,128)S(1)} %reshape.63), channel_id=1, replica_groups=mesh['slab'=4,'grp'=8] {'grp'}, dimensions={0}, use_global_device_ids=true | all-gather | bytes 64512 | tf_op jit(solution)/shard_map/all_gather | solution.py:96
  48.9 12.9 %maximum_convert_fusion = f32[32,18,10752]{2,0,1:T(8,128)} fusion(bf16[32,3,10752]{2,0,1:T(8,128)(2,1)} %collective-permute-done.1, bf16[32,12,10752]{2,0,1:T(8,128)(2,1)} %param.4, bf16[32,3,10752]{2,0,1:T(8,128)(2,1)S(1)} %collective-permute-done), kind=kLoop, calls=%fused_computation.29 | loop fusion | flops 18579456 | bytes 37158912 | tf_op jit(solution)/shard_map/convert_element_type | solution.py:100
  61.8 64.2 %multiply_add_fusion.1 = f32[32,18,10752]{2,0,1:T(8,128)} fusion(f32[32,18,10752]{2,0,1:T(8,128)} %maximum_convert_fusion, pred[10752]{0:T(1024)(128)(4,1)S(1)} %get-tuple-element.8, pred[10752]{0:T(1024)(128)(4,1)S(1)} %get-tuple-element.9, pred[10752]{0:T(1024)(128)(4,1)S(1)} %get-tuple-element.10, pred[10752]{0:T(1024)(128)(4,1)S(1)} %fusion.58, ...), kind=kLoop, calls=%fused_computation.7 | loop fusion | flops 123863040 | bytes 49620480 | tf_op jit(solution)/shard_map/add | solution.py:52
  125.9 64.0 %multiply_add_fusion = f32[32,18,10752]{2,0,1:T(8,128)} fusion(f32[32,18,10752]{2,0,1:T(8,128)} %multiply_add_fusion.1), kind=kLoop, calls=%fused_computation.1 | loop fusion | flops 80510976 | bytes 49545216 | tf_op jit(solution)/shard_map/add | solution.py:65
  189.9 40.4 %fusion.9 = bf16[32,12,10752]{2,0,1:T(8,128)(2,1)} fusion(f32[32,18,10752]{2,0,1:T(8,128)} %multiply_add_fusion), kind=kLoop, calls=%fused_computation.17 | loop fusion | flops 57802752 | bytes 123863040 | tf_op jit(solution)/shard_map/convert_element_type | solution.py:104
  230.3 12.2 %copy.23 = bf16[32,12,10752]{2,1,0:T(8,128)(2,1)} copy(bf16[32,12,10752]{2,0,1:T(8,128)(2,1)} %fusion.9) | data formatting | bytes 16515072 | tf_op jit(solution)/shard_map/convert_element_type | solution.py:104
  242.5 18.6 %convert_element_type.54 = bf16[32,1008,128]{2,1,0:T(8,128)(2,1)} reshape(bf16[32,12,10752]{2,1,0:T(8,128)(2,1)} %copy.23) | data formatting | bytes 16515072 | tf_op jit(solution)/shard_map/convert_element_type | solution.py:104
  261.0 8.6 %copy.24 = bf16[32,1008,128]{2,0,1:T(8,128)(2,1)} copy(bf16[32,1008,128]{2,1,0:T(8,128)(2,1)} %convert_element_type.54) | data formatting | bytes 16515072 | tf_op jit(solution)/shard_map/convert_element_type | solution.py:104
  269.7 4.1 gather_fusion
  274.1 1.0 gather.7
  275.4 24.6 %all_to_all.10 = bf16[32,8,1792]{2,0,1:T(8,128)(2,1)S(1)} all-to-all(bf16[32,8,1792]{2,0,1:T(8,128)(2,1)S(1)} %copy.26), channel_id=1, replica_groups=mesh['slab'=4,'grp'=8] {'grp'}, dimensions={1} | all-to-all | bytes 1835008 | tf_op jit(solution)/shard_map/all_to_all | solution.py:107
  300.5 14.3 %fusion.19 = f32[1456,1456]{1,0:T(8,128)} fusion(bf16[256,1792]{1,0:T(8,128)(2,1)S(1)} %fusion.24, bf16[1200,1792]{1,0:T(8,128)(2,1)} %param.6), kind=kOutput, calls=%fused_computation.37 | convolution fusion | flops 7608287232 | bytes 13698048 | tf_op jit(solution)/shard_map/dot_general | solution.py:119
  314.9 0.4 multiply_reduce_fusion
  315.5 40.8 %psum.15 = f32[2]{0:T(128)S(1)} all-reduce(f32[2]{0:T(128)S(1)} %reduce_sum.37), channel_id=1, replica_groups=mesh['slab'=4,'grp'=8] {'slab','grp'}, use_global_device_ids=true, to_apply=%region_5.6 | all-reduce | flops 2 | bytes 16 | tf_op jit(solution)/shard_map/psum | solution.py:115
  356.7 0.6 fusion.62
  357.4 3.5 fusion.16
  360.9 3.1 fusion.17
  364.0 9.7 %fusion.18 = bf16[1200,1792]{1,0:T(8,128)(2,1)} fusion(f32[1200,1792]{1,0:T(8,128)S(1)} %fusion.17, f32[1200,1792]{1,0:T(8,128)S(1)} %fusion.16, bf16[1200,1792]{1,0:T(8,128)(2,1)} %param.6, bf16[1456,1200]{0,1:T(8,128)(2,1)S(1)} %copy-done), kind=kOutput, calls=%fused_computation.36 | convolution fusion | flops 5167411200 | bytes 28876800 | tf_op jit(solution)/shard_map/dot_general | solution.py:127
  373.7 128.2 %all-reduce.5.cloned.1.call-done = f32[1456,1456]{1,0:T(8,128)} async-done(((f32[1456,1456]{1,0:T(8,128)}), f32[1456,1456]{1,0:T(8,128)}) %all-reduce.5.cloned.1.call-update) | async-done | bytes 8479760 | tf_op jit(solution)/shard_map/psum | solution.py:118
  501.9 2.5 multiply_multiply_fusion
  (35 shorter events, 2.5 us)
Async XLA Ops:
  7.2 494.8 %all-reduce.5.cloned.1.call-start = ((), (), s32[]{:S(2)}) async-start(), calls=%async_computation.1 | async-start | bytes 17891328 | tf_op jit(solution)/shard_map/psum | solution.py:118
  11.7 37.2 %collective-permute-start = (bf16[32,3,10752]{2,0,1:T(8,128)(2,1)}, bf16[32,3,10752]{2,0,1:T(8,128)(2,1)S(1)}, u32[]{:S(2)}, u32[]{:S(2)}) collective-permute-start(bf16[32,3,10752]{2,0,1:T(8,128)(2,1)} %get-tuple-element.4), channel_id=1, source_target_pairs={{0,8},{8,16},{16,24},{1,9},{9,17},{17,25},{2,10},{10,18},{18,26},{... | collective-permute-start | bytes 6193160 | tf_op jit(solution)/shard_map/ppermute | solution.py:23
  14.2 34.6 %collective-permute-start.1 = (bf16[32,3,10752]{2,0,1:T(8,128)(2,1)}, bf16[32,3,10752]{2,0,1:T(8,128)(2,1)}, u32[]{:S(2)}, u32[]{:S(2)}) collective-permute-start(bf16[32,3,10752]{2,0,1:T(8,128)(2,1)} %get-tuple-element.5), channel_id=1, source_target_pairs={{8,0},{16,8},{24,16},{9,1},{17,9},{25,17},{10,2},{18,10},{26,18},{... | collective-permute-start | bytes 6193160 | tf_op jit(solution)/shard_map/ppermute | solution.py:25
  357.4 6.6 %copy-start = (bf16[1456,1200]{0,1:T(8,128)(2,1)S(1)}, bf16[1456,1200]{0,1:T(8,128)(2,1)}, u32[]{:S(2)}) copy-start(bf16[1456,1200]{0,1:T(8,128)(2,1)} %param.7) | copy-start | bytes 10483204
Sparse Core Ops, SparseCore 0:
  315.0 186.8 all-reduce.4
where the time goes:
time: 512 us; the launch traced here: 511 us
  other arithmetic  186 us (36%)
  waiting for transfers between devices  128 us (25%)
  blocking collectives  97.3 us (19%)
  local copies, waits for them, and re-layouts  51.4 us (10%)
  matrix products  30.6 us (6%)
  between operations  14.2 us (3%)
    psum x1, waiting for transfers between devices, body(): lax.psum(jnp.dot(stacked, stacked.T, preferred_element_type=jnp.float32),...  128 us
    add x1, other arithmetic, along_rows(): summed = summed + weights[offset + RAD] * jnp.where(inside, shifted, 0.0)  64.2 us
    add x1, other arithmetic, along_columns(): summed = summed + weights[offset + RAD] * shifted  64 us
    psum x1, blocking collectives, body(): power = lax.psum(jnp.sum(widened * widened, axis=(1, 2)), ('slab', 'grp'))  40.8 us
    convert_element_type x1, other arithmetic, body(): smoothed = along_depth(planar, slab_depth).reshape(frames_here, slab_dept...  40.4 us
    convert_element_type x3, local copies, waits for them, and re-layouts, body(): smoothed = along_depth(planar, slab_depth).reshape(frames_here, slab_dept...  39.4 us
    all_gather x1, blocking collectives, body(): lax.all_gather(mask_index, 'grp', axis=0, tiled=True)  31.9 us
    all_to_all x1, blocking collectives, body(): lax.all_to_all(picked, 'grp', split_axis=1, concat_axis=0, tiled=True)  24.6 us
  transfers between devices with their start and end apart: 3, of which 1 were waited for; matrix products, arithmetic and copies ran while one was open for 4% of the time, Pallas kernels for 0%

commit v1 on v0

--- a/solution.py
+++ b/solution.py
@@ -3,6 +3,7 @@
 import jax.numpy as jnp
 from jax import lax
 from jax.sharding import PartitionSpec as P
+from jax.lax import psum
 
 NX = 96
 RUN = 128
@@ -115,9 +116,8 @@
     power = lax.psum(jnp.sum(widened * widened, axis=(1, 2)), ("slab", "grp"))
     rows_here = order_rows // group_count
     first_row = lax.axis_index("grp") * rows_here
-    gram_raw = lax.psum(
-        jnp.dot(stacked, stacked.T, preferred_element_type=jnp.float32), ("slab", "grp")
-    )
+    target_get = lambda sheet: psum(psum(sheet, axis_name="grp"), axis_name="slab")
+    gram_raw = target_get(jnp.dot(stacked, stacked.T, preferred_element_type=jnp.float32))
     owned = lax.dynamic_slice_in_dim(gram_raw, first_row, rows_here, 0)
     scales = lax.rsqrt(power / (masked * subject_frames) + epsilon)
     row_scale = jnp.concatenate([jnp.ones((K,), jnp.float32), jnp.repeat(scales, subject_frames)])

time: 512 us -> 774 us (1.51)
  waiting for transfers between devices: 128 us -> 390 us
    psum x1 -> x2, waiting for transfers between devices: 128 us -> 390 us  [the longest x1 284 us: body(): psum(sheet, axis_name='grp')]
  transfers between devices with their start and end apart: 3 -> 4, of which waited for: 1 -> 2; matrix products, arithmetic and copies ran while one was open for 4% -> 2% of each run, Pallas kernels for 0% -> 0%
where the time goes in v1:
time: 774 us; the launch traced here: 773 us
  waiting for transfers between devices  390 us (50%)
  other arithmetic  186 us (24%)
  blocking collectives  97.1 us (13%)
  local copies, waits for them, and re-layouts  51.4 us (7%)
  matrix products  30.4 us (4%)
  between operations  14.3 us (2%)
    psum x1, waiting for transfers between devices, body(): psum(sheet, axis_name='grp')  284 us
    psum x1, waiting for transfers between devices, body(): psum(psum(sheet, axis_name='grp'), axis_name='slab')  106 us
    add x1, other arithmetic, along_rows(): summed = summed + weights[offset + RAD] * jnp.where(inside, shifted, 0.0)  64.2 us
    add x1, other arithmetic, along_columns(): summed = summed + weights[offset + RAD] * shifted  64 us
    psum x1, blocking collectives, body(): power = lax.psum(jnp.sum(widened * widened, axis=(1, 2)), ('slab', 'grp'))  40.6 us
    convert_element_type x1, other arithmetic, body(): smoothed = along_depth(planar, slab_depth).reshape(frames_here, slab_dept...  40.4 us
    convert_element_type x3, local copies, waits for them, and re-layouts, body(): smoothed = along_depth(planar, slab_depth).reshape(frames_here, slab_dept...  39.4 us
    all_gather x1, blocking collectives, body(): lax.all_gather(mask_index, 'grp', axis=0, tiled=True)  31.9 us
  transfers between devices with their start and end apart: 4, of which 2 were waited for; matrix products, arithmetic and copies ran while one was open for 2% of the time, Pallas kernels for 0%

profile of v1, /device:TPU:0, one launch (start us, length us, event | category | flops | bytes accessed | tf_op | source)
XLA Modules:
  0.0 772.7 jit_solution(17878890378840630101)
XLA Ops:
  7.2 4.5 fusion.61
  11.7 2.5 collective-permute-start
  14.2 1.3 collective-permute-start.1
  15.5 0.7 reshape.63
  16.2 31.9 %all-gather = s32[8,1,1792]{2,1,0:T(1,128)S(1)} all-gather(s32[1,1,1792]{2,1,0:T(1,128)S(1)} %reshape.63), channel_id=1, replica_groups=mesh['slab'=4,'grp'=8] {'grp'}, dimensions={0}, use_global_device_ids=true | all-gather | bytes 64512 | tf_op jit(solution)/shard_map/all_gather | solution.py:97
  48.9 12.9 %maximum_convert_fusion = f32[32,18,10752]{2,0,1:T(8,128)} fusion(bf16[32,3,10752]{2,0,1:T(8,128)(2,1)} %collective-permute-done.1, bf16[32,12,10752]{2,0,1:T(8,128)(2,1)} %param.4, bf16[32,3,10752]{2,0,1:T(8,128)(2,1)S(1)} %collective-permute-done), kind=kLoop, calls=%fused_computation.29 | loop fusion | flops 18579456 | bytes 37158912 | tf_op jit(solution)/shard_map/convert_element_type | solution.py:101
  61.8 64.2 %multiply_add_fusion.1 = f32[32,18,10752]{2,0,1:T(8,128)} fusion(f32[32,18,10752]{2,0,1:T(8,128)} %maximum_convert_fusion, pred[10752]{0:T(1024)(128)(4,1)S(1)} %get-tuple-element.8, pred[10752]{0:T(1024)(128)(4,1)S(1)} %get-tuple-element.9, pred[10752]{0:T(1024)(128)(4,1)S(1)} %get-tuple-element.10, pred[10752]{0:T(1024)(128)(4,1)S(1)} %fusion.58, ...), kind=kLoop, calls=%fused_computation.7 | loop fusion | flops 123863040 | bytes 49620480 | tf_op jit(solution)/shard_map/add | solution.py:53
  125.9 64.0 %multiply_add_fusion = f32[32,18,10752]{2,0,1:T(8,128)} fusion(f32[32,18,10752]{2,0,1:T(8,128)} %multiply_add_fusion.1), kind=kLoop, calls=%fused_computation.1 | loop fusion | flops 80510976 | bytes 49545216 | tf_op jit(solution)/shard_map/add | solution.py:66
  189.9 40.4 %fusion.9 = bf16[32,12,10752]{2,0,1:T(8,128)(2,1)} fusion(f32[32,18,10752]{2,0,1:T(8,128)} %multiply_add_fusion), kind=kLoop, calls=%fused_computation.17 | loop fusion | flops 57802752 | bytes 123863040 | tf_op jit(solution)/shard_map/convert_element_type | solution.py:105
  230.3 12.2 %copy.23 = bf16[32,12,10752]{2,1,0:T(8,128)(2,1)} copy(bf16[32,12,10752]{2,0,1:T(8,128)(2,1)} %fusion.9) | data formatting | bytes 16515072 | tf_op jit(solution)/shard_map/convert_element_type | solution.py:105
  242.5 18.6 %convert_element_type.54 = bf16[32,1008,128]{2,1,0:T(8,128)(2,1)} reshape(bf16[32,12,10752]{2,1,0:T(8,128)(2,1)} %copy.23) | data formatting | bytes 16515072 | tf_op jit(solution)/shard_map/convert_element_type | solution.py:105
  261.0 8.6 %copy.24 = bf16[32,1008,128]{2,0,1:T(8,128)(2,1)} copy(bf16[32,1008,128]{2,1,0:T(8,128)(2,1)} %convert_element_type.54) | data formatting | bytes 16515072 | tf_op jit(solution)/shard_map/convert_element_type | solution.py:105
  269.7 4.1 gather_fusion
  274.1 1.0 gather.7
  275.4 24.6 %all_to_all.10 = bf16[32,8,1792]{2,0,1:T(8,128)(2,1)S(1)} all-to-all(bf16[32,8,1792]{2,0,1:T(8,128)(2,1)S(1)} %copy.26), channel_id=1, replica_groups=mesh['slab'=4,'grp'=8] {'grp'}, dimensions={1} | all-to-all | bytes 1835008 | tf_op jit(solution)/shard_map/all_to_all | solution.py:108
  300.5 14.3 %fusion.19 = f32[1456,1456]{1,0:T(8,128)} fusion(bf16[256,1792]{1,0:T(8,128)(2,1)S(1)} %fusion.24, bf16[1200,1792]{1,0:T(8,128)(2,1)} %param.6), kind=kOutput, calls=%fused_computation.37 | convolution fusion | flops 7608287232 | bytes 13698048 | tf_op jit(solution)/shard_map/dot_general | solution.py:120
  314.9 283.8 %all-reduce.6.cloned.1.call-done = f32[1456,1456]{1,0:T(8,128)} async-done(((f32[1456,1456]{1,0:T(8,128)}), f32[1456,1456]{1,0:T(8,128)}) %all-reduce.6.cloned.1.call-update) | async-done | bytes 8479760 | tf_op jit(solution)/shard_map/psum | solution.py:119
  599.3 40.6 %psum.23 = f32[2]{0:T(128)S(1)} all-reduce(f32[2]{0:T(128)S(1)} %reduce_sum.37), channel_id=1, replica_groups=mesh['slab'=4,'grp'=8] {'slab','grp'}, use_global_device_ids=true, to_apply=%region_6.7 | all-reduce | flops 2 | bytes 16 | tf_op jit(solution)/shard_map/psum | solution.py:116
  640.3 0.6 fusion.62
  641.0 3.4 fusion.16
  644.4 3.1 fusion.17
  647.5 9.7 %fusion.18 = bf16[1200,1792]{1,0:T(8,128)(2,1)} fusion(f32[1200,1792]{1,0:T(8,128)S(1)} %fusion.17, f32[1200,1792]{1,0:T(8,128)S(1)} %fusion.16, bf16[1200,1792]{1,0:T(8,128)(2,1)} %param.6, bf16[1456,1200]{0,1:T(8,128)(2,1)S(1)} %copy-done), kind=kOutput, calls=%fused_computation.36 | convolution fusion | flops 5167411200 | bytes 28876800 | tf_op jit(solution)/shard_map/dot_general | solution.py:127
  657.1 106.2 %all-reduce.8.cloned.1.call-done = f32[1456,1456]{1,0:T(8,128)} async-done(((f32[1456,1456]{1,0:T(8,128)}), f32[1456,1456]{1,0:T(8,128)}) %all-reduce.8.cloned.1.call-update) | async-done | bytes 8479760 | tf_op jit(solution)/shard_map/psum | solution.py:119
  763.3 2.5 multiply_multiply_fusion
  (38 shorter events, 3.0 us)
Async XLA Ops:
  7.2 591.5 %all-reduce.6.cloned.1.call-start = ((), (), s32[]{:S(2)}) async-start(), calls=%async_computation.1 | async-start | bytes 17891328 | tf_op jit(solution)/shard_map/psum | solution.py:119
  11.7 37.2 %collective-permute-start = (bf16[32,3,10752]{2,0,1:T(8,128)(2,1)}, bf16[32,3,10752]{2,0,1:T(8,128)(2,1)S(1)}, u32[]{:S(2)}, u32[]{:S(2)}) collective-permute-start(bf16[32,3,10752]{2,0,1:T(8,128)(2,1)} %get-tuple-element.4), channel_id=1, source_target_pairs={{0,8},{8,16},{16,24},{1,9},{9,17},{17,25},{2,10},{10,18},{18,26},{... | collective-permute-start | bytes 6193160 | tf_op jit(solution)/shard_map/ppermute | solution.py:24
  14.2 34.6 %collective-permute-start.1 = (bf16[32,3,10752]{2,0,1:T(8,128)(2,1)}, bf16[32,3,10752]{2,0,1:T(8,128)(2,1)}, u32[]{:S(2)}, u32[]{:S(2)}) collective-permute-start(bf16[32,3,10752]{2,0,1:T(8,128)(2,1)} %get-tuple-element.5), channel_id=1, source_target_pairs={{8,0},{16,8},{24,16},{9,1},{17,9},{25,17},{10,2},{18,10},{26,18},{... | collective-permute-start | bytes 6193160 | tf_op jit(solution)/shard_map/ppermute | solution.py:26
  314.9 448.5 %all-reduce.8.cloned.1.call-start = ((), (), s32[]{:S(2)}) async-start(), calls=%async_computation.2 | async-start | bytes 17891328 | tf_op jit(solution)/shard_map/psum | solution.py:119
  641.0 6.5 copy-start
Sparse Core Ops, SparseCore 0:
  315.0 283.6 all-reduce.5
  601.1 162.1 all-reduce.7
